TPU v7x, 128 devices: a whole 4x4x4 slice. The times are simulated.
128 devices in a mesh: dp: 8 (over x_hi, z), expert: 16 (over y, x_lo, core).
Axes of the slice: x: 4 (x_hi: 2, x_lo: 2; x = x_hi * 2 + x_lo), y: 4, z: 4, core: 2. Of those that a mesh axis runs over, the one named last changes fastest.
Arguments:
- tokens: bfloat16 [32768, 2048], P(('dp', 'expert')), may hold values from -6 to 6
- expert_ids: int32 [32768, 4], P(('dp', 'expert')), may hold values from 0 to 15, as said below
- gates: float32 [32768, 4], P(('dp', 'expert')), may hold values from 0.1 to 1
- w_gate: bfloat16 [16, 2048, 384], P('expert'), may hold values from -0.125 to 0.125
- w_up: bfloat16 [16, 2048, 384], P('expert'), may hold values from -0.125 to 0.125
- w_down: bfloat16 [16, 2048, 384], P('expert'), may hold values from -0.3125 to 0.3125
- cotangent: bfloat16 [32768, 2048], P(('dp', 'expert')), may hold values from -6 to 6
Outputs:
- mixed: bfloat16 [32768, 2048], P(('dp', 'expert'))
- tokens_grad: bfloat16 [32768, 2048], P(('dp', 'expert'))
- gates_grad: float32 [32768, 4], P(('dp', 'expert'))
- gate_grad: float32 [16, 2048, 384], P('expert', 'dp')
- up_grad: float32 [16, 2048, 384], P('expert', 'dp')
- down_grad: float32 [16, 2048, 384], P('expert', 'dp')
Inputs may be any that keep to these rules, and one draw needn't show every extreme that they name: `expert_ids`: each row holds 4 different experts. One expert, the same in every draw position, is named by every token. Among the 256 tokens of one device every other expert is named at most 52 times, and one of them is named exactly 52 times on every device.
All inputs are finite; a program needn't handle non-finite values.
Results may differ from a plain program's by a relative error of at most 0.014.
Values may be sent and summed in bfloat16 or wider, within the bound.
A program may use at most 128 MiB of HBM per device.

v0:
```python
import jax
import jax.numpy as jnp
from jax import lax
from jax.sharding import PartitionSpec as P

D = 2048
FF = 384
TOPK = 4


def broadcast(value, axis, source):
    kept = jnp.where(lax.axis_index(axis) == source, value, 0).astype(value.dtype)
    return lax.psum(kept, axis)


def expert_forward(rows, weight_gate, weight_up, weight_down):
    gate_act = jnp.dot(rows, weight_gate, preferred_element_type=jnp.float32)
    up_act = jnp.dot(rows, weight_up, preferred_element_type=jnp.float32)
    hidden = (jax.nn.silu(gate_act) * up_act).astype(jnp.bfloat16)
    output = lax.dot_general(
        hidden, weight_down, (((1,), (1,)), ((), ())), preferred_element_type=jnp.float32
    ).astype(jnp.bfloat16)
    return (gate_act, up_act, hidden, output)


def expert_backward(rows, upstream, weight_gate, weight_up, weight_down, gate_act, up_act, hidden):
    hidden_grad = jnp.dot(upstream, weight_down, preferred_element_type=jnp.float32)
    sigma = jax.nn.sigmoid(gate_act)
    gate_pre = (hidden_grad * up_act * sigma * (1.0 + gate_act * (1.0 - sigma))).astype(
        jnp.bfloat16
    )
    up_pre = (hidden_grad * gate_act * sigma).astype(jnp.bfloat16)
    contract = (((1,), (1,)), ((), ()))
    input_part = (
        lax.dot_general(gate_pre, weight_gate, contract, preferred_element_type=jnp.float32)
        + lax.dot_general(up_pre, weight_up, contract, preferred_element_type=jnp.float32)
    ).astype(jnp.bfloat16)
    over_rows = (((0,), (0,)), ((), ()))
    grad_gate = lax.dot_general(rows, gate_pre, over_rows, preferred_element_type=jnp.float32)
    grad_upper = lax.dot_general(rows, up_pre, over_rows, preferred_element_type=jnp.float32)
    grad_down = lax.dot_general(upstream, hidden, over_rows, preferred_element_type=jnp.float32)
    return (input_part, grad_gate, grad_upper, grad_down)


def per_device(tokens, expert_ids, gates, w_gate, w_up, w_down, cotangent):
    experts = lax.axis_size("expert")
    tok_rows = tokens.shape[0]
    capacity = (tok_rows * (TOPK - 1) + experts - 2) // (experts - 1)
    over_rows = (((0,), (0,)), ((), ()))
    highest = lax.Precision.HIGHEST
    expert_range = jnp.arange(experts, dtype=jnp.int32)
    matches = (expert_ids[:, :, None] == expert_range).astype(jnp.int32)
    counts = jnp.sum(matches, axis=(0, 1))
    hot_expert = jnp.argmax(counts)
    is_hot = expert_ids == hot_expert
    flat_matches = matches.reshape(tok_rows * TOPK, experts)
    before = jnp.cumsum(flat_matches, axis=0) - flat_matches
    position = jnp.sum(before * flat_matches, axis=1)
    target = jnp.where(is_hot.reshape(-1), -1, expert_ids.reshape(-1) * capacity + position)
    slot_ids = jnp.arange(experts * capacity, dtype=jnp.int32)
    dispatch_f = (slot_ids[:, None] == target[None, :]).astype(jnp.float32)
    per_token_f = jnp.sum(dispatch_f.reshape(experts * capacity, tok_rows, TOPK), axis=2)
    per_token = per_token_f.astype(jnp.bfloat16)
    slot_gate = jnp.dot(
        dispatch_f, gates.reshape(-1), precision=highest, preferred_element_type=jnp.float32
    )
    own_weights = (w_gate[0], w_up[0], w_down[0])
    shadow = (
        broadcast(own_weights[0], "expert", hot_expert),
        broadcast(own_weights[1], "expert", hot_expert),
        broadcast(own_weights[2], "expert", hot_expert),
    )
    outgoing = jnp.dot(per_token, tokens, preferred_element_type=jnp.float32).astype(jnp.bfloat16)
    outgoing = outgoing.reshape(experts, capacity, D)
    rows = lax.all_to_all(outgoing, "expert", split_axis=0, concat_axis=0, tiled=True)
    leading = rows.shape[:2]
    gate_act, up_act, hidden, output = expert_forward(rows.reshape(-1, D), *own_weights)
    received, expert_out, gate_act, up_act, hidden = (
        rows,
        output.reshape(leading + (D,)),
        gate_act.reshape(leading + (FF,)),
        up_act.reshape(leading + (FF,)),
        hidden.reshape(leading + (FF,)),
    )
    returned = lax.all_to_all(expert_out, "expert", split_axis=0, concat_axis=0, tiled=True)
    hot_gate, hot_up, hot_hidden, hot_out = expert_forward(tokens, *shadow)
    returned_f = returned.reshape(-1, D).astype(jnp.float32)
    weighted = slot_gate[:, None] * returned_f
    mixed_cold = lax.dot_general(
        per_token_f, weighted, over_rows, precision=highest, preferred_element_type=jnp.float32
    )
    hot_weight = jnp.sum(jnp.where(is_hot, gates, 0.0), axis=1)
    hot_out_f = hot_out.astype(jnp.float32)
    mixed = (mixed_cold + hot_weight[:, None] * hot_out_f).astype(jnp.bfloat16)
    upstream = cotangent.astype(jnp.float32)
    copied = jnp.dot(per_token, cotangent, preferred_element_type=jnp.float32)
    slot_dot = jnp.sum(returned_f * copied, axis=1)
    cold_gates = jnp.dot(
        slot_dot, dispatch_f, precision=highest, preferred_element_type=jnp.float32
    ).reshape(tok_rows, TOPK)
    hot_dot = jnp.sum(upstream * hot_out_f, axis=1)
    gates_grad = cold_gates + jnp.where(is_hot, hot_dot[:, None], 0.0)
    outgoing_grad = (slot_gate[:, None] * copied).astype(jnp.bfloat16)
    incoming_grad = lax.all_to_all(
        outgoing_grad.reshape(experts, capacity, D),
        "expert",
        split_axis=0,
        concat_axis=0,
        tiled=True,
    )
    input_rows, own_gate, own_upper, own_down = expert_backward(
        received.reshape(-1, D),
        incoming_grad.reshape(-1, D),
        *own_weights,
        gate_act.reshape(-1, FF),
        up_act.reshape(-1, FF),
        hidden.reshape(-1, FF)
    )
    back_rows = lax.all_to_all(
        input_rows.reshape(experts, capacity, D), "expert", split_axis=0, concat_axis=0, tiled=True
    )
    cold_input = lax.dot_general(
        per_token, back_rows.reshape(-1, D), over_rows, preferred_element_type=jnp.float32
    )
    hot_upstream = (hot_weight[:, None] * upstream).astype(jnp.bfloat16)
    hot_input, hot_gate_grad, hot_upper_grad, hot_down_grad = expert_backward(
        tokens, hot_upstream, *shadow, hot_gate, hot_up, hot_hidden
    )
    tokens_grad = (cold_input + hot_input.astype(jnp.float32)).astype(jnp.bfloat16)
    own_part = jnp.stack([own_gate, own_upper, own_down])
    hot_part = jnp.stack([hot_gate_grad, hot_upper_grad, hot_down_grad])
    is_owner = lax.axis_index("expert") == hot_expert
    hot_total = lax.psum(hot_part.astype(jnp.bfloat16), "expert").astype(jnp.float32)
    grads = lax.psum_scatter(
        own_part + jnp.where(is_owner, hot_total, 0.0), "dp", scatter_dimension=1, tiled=True
    )
    return (mixed, tokens_grad, gates_grad, grads[0][None], grads[1][None], grads[2][None])


def solution(mesh):
    return jax.shard_map(
        per_device,
        mesh=mesh,
        in_specs=(
            P(("dp", "expert"), None),
            P(("dp", "expert"), None),
            P(("dp", "expert"), None),
            P("expert", None, None),
            P("expert", None, None),
            P("expert", None, None),
            P(("dp", "expert"), None),
        ),
        out_specs=(
            P(("dp", "expert"), None),
            P(("dp", "expert"), None),
            P(("dp", "expert"), None),
            P("expert", "dp", None),
            P("expert", "dp", None),
            P("expert", "dp", None),
        ),
        check_vma=False,
    )
```

profile of v0, /device:TPU:0, one launch (start us, length us, event | category | flops | bytes accessed | tf_op | source)
XLA Modules:
  0.0 584.9 jit_solution(7026955467745829882)
XLA Ops:
  7.2 0.9 convert_reduce_fusion.1
  9.8 4.5 reduce-window.6
  15.0 1.4 select_reduce_fusion.1
  17.6 2.8 convolution_convert_fusion.1
  20.4 4.6 reshape.98
  25.0 5.7 all-to-all-start
  31.5 2.9 bitcast_select_fusion
  34.4 2.1 bitcast_select_fusion.1
  36.6 62.9 %all-to-all-done = bf16[16,52,2048]{2,1,0:T(8,128)(2,1)} async-done(((bf16[16,52,2048]{2,1,0:T(8,128)(2,1)}), bf16[16,52,2048]{2,1,0:T(8,128)(2,1)}, u32[]{:S(2)}, u32[]{:S(2)}) %all-to-all-start) | async-done | bytes 3407904 | tf_op jit(solution)/shard_map/all_to_all | solution.py:75
  99.4 4.7 reshape.99
  104.1 4.5 fusion.28
  108.7 3.0 multiply_convert_fusion.3
  111.7 0.8 copy-done.23
  112.5 3.7 convolution_convert_fusion
  116.2 4.6 reshape.100
  120.8 5.1 all-to-all-start.1
  126.5 1.6 fusion.30
  128.1 92.6 %all-reduce.6.cloned.1.call-done = (bf16[2048,384]{1,0:T(8,128)(2,1)}, bf16[2048,384]{1,0:T(8,128)(2,1)}, bf16[2048,384]{1,0:T(8,128)(2,1)}) async-done(((bf16[2048,384]{1,0:T(8,128)(2,1)}, bf16[2048,384]{1,0:T(8,128)(2,1)}, bf16[2048,384]{1,0:T(8,128)(2,1)}), (bf16[2048,384]{1,0:T(8,128)(2,1)}, bf16[2048,384]{1,0:T(8,128)(2,1)}, bf16[2048,384]{1,0:T(8,128)(2,1)})) %all-reduce.6.cloned.1.call-update) | async-done | bytes 4718608 | tf_op jit(solution)/shard_map/psum | solution.py:13
  220.8 2.1 convolution_bitcast_fusion.4
  224.6 1.0 multiply_convert_fusion.4
  225.6 1.9 fusion.9
  227.5 2.0 fusion.10
  229.6 5.4 reshape.105
  235.0 5.8 multiply_reduce_fusion
  240.8 4.5 reshape.101
  245.3 4.5 all-to-all-start.2
  251.3 3.6 pad_maximum_fusion
  255.1 63.2 %all-to-all-done.2 = bf16[16,52,2048]{2,1,0:T(8,128)(2,1)} async-done(((bf16[16,52,2048]{2,1,0:T(8,128)(2,1)}), bf16[16,52,2048]{2,1,0:T(8,128)(2,1)}, u32[]{:S(2)}, u32[]{:S(2)}) %all-to-all-start.2) | async-done | bytes 3407904 | tf_op jit(solution)/shard_map/all_to_all | solution.py:104
  318.4 4.6 reshape.102
  323.0 6.2 %convolution_bitcast_fusion = f32[1,2048,384]{2,1,0:T(8,128)} fusion(bf16[832,2048]{1,0:T(8,128)(2,1)} %reshape.102, bf16[832,384]{1,0:T(8,128)(2,1)S(1)} %copy-done.24), kind=kOutput, calls=%fused_computation.17 | convolution fusion | flops 1308622848 | bytes 7192576 | tf_op jit(solution)/shard_map/dot_general | solution.py:41
  329.2 2.3 multiply_convert_fusion.1
  331.5 4.0 convolution_bitcast_fusion.1
  335.5 4.0 convolution_bitcast_fusion.2
  339.5 77.1 %all-reduce.4.cloned.1.call-done = bf16[3,2048,384]{2,1,0:T(8,128)(2,1)} async-done(((bf16[3,2048,384]{2,1,0:T(8,128)(2,1)}), bf16[3,2048,384]{2,1,0:T(8,128)(2,1)}) %all-reduce.4.cloned.1.call-update) | async-done | bytes 4718608 | tf_op jit(solution)/shard_map/psum | solution.py:133
  416.6 9.4 %maximum_add_fusion = f32[3,2048,384]{2,1,0:T(8,128)} fusion(f32[1,2048,384]{2,1,0:T(8,128)} %convolution_bitcast_fusion, f32[1,2048,384]{2,1,0:T(8,128)} %convolution_bitcast_fusion.1, f32[1,2048,384]{2,1,0:T(8,128)} %convolution_bitcast_fusion.2, bf16[3,2048,384]{2,1,0:T(8,128)(2,1)} %all-reduce.4.cloned.1.call-done, pred[]{:T(512)S(6)} %eq.93), kind=kLoop, calls=%fused_computation | loop fusion | flops 11796480 | bytes 23592960 | tf_op jit(solution)/shard_map/add | solution.py:135
  426.0 3.5 fusion.26
  429.5 3.7 add_convert_fusion
  433.2 4.7 reshape.103
  437.9 4.5 all-to-all-start.3
  443.2 2.9 fusion.18
  447.6 2.2 fusion.16
  449.8 1.7 select_reduce_fusion
  452.2 10.3 %fusion.11 = bf16[256,2048]{1,0:T(8,128)(2,1)} fusion(f32[832,256]{1,0:T(8,128)S(1)} %convert_reduce_fusion, f32[832,2048]{1,0:T(8,128)} %reshape.105, f32[832]{0:T(1024)S(1)} %fusion.30, bf16[256,2048]{1,0:T(8,128)(2,1)S(1)} %get-tuple-element.38, f32[256]{0:T(256)S(1)} %get-tuple-element.23), kind=kOutput, calls=%fused_computation.32 | convolution fusion | flops 5238292480 | bytes 9769216 | tf_op jit(solution)/shard_map/dot_general | solution.py:89
  462.5 46.8 %all-to-all-done.3 = bf16[16,52,2048]{2,1,0:T(8,128)(2,1)} async-done(((bf16[16,52,2048]{2,1,0:T(8,128)(2,1)}), bf16[16,52,2048]{2,1,0:T(8,128)(2,1)}, u32[]{:S(2)}, u32[]{:S(2)}) %all-to-all-start.3) | async-done | bytes 3407904 | tf_op jit(solution)/shard_map/all_to_all | solution.py:119
  509.2 4.6 reshape.104
  513.8 4.9 fusion.14
  518.7 57.2 %reduce-scatter.2.cloned.1.call-done = f32[3,256,384]{2,1,0:T(8,128)} async-done(((f32[3,2048,384]{2,1,0:T(8,128)}), f32[3,256,384]{2,1,0:T(8,128)}) %reduce-scatter.2.cloned.1.call-update) | async-done | bytes 1179664 | tf_op jit(solution)/shard_map/reduce_scatter | solution.py:134
  575.9 2.3 fusion.42
  (89 shorter events, 10.6 us)
Async XLA Ops:
  7.2 10.4 %copy-start = (bf16[256,2048]{1,0:T(8,128)(2,1)S(1)}, bf16[256,2048]{1,0:T(8,128)(2,1)}, u32[]{:S(2)}) copy-start(bf16[256,2048]{1,0:T(8,128)(2,1)} %param.7) | copy-start | bytes 3145732
  16.4 109.7 %copy-start.20 = (pred[256,4]{0,1:T(4,128)(4,1)}, pred[256,4]{0,1:T(4,128)(4,1)S(1)}, u32[]{:S(2)}) copy-start(pred[256,4]{0,1:T(4,128)(4,1)S(1)} %get-tuple-element.24) | copy-start | bytes 3076
  25.0 74.5 %all-to-all-start = ((bf16[16,52,2048]{2,1,0:T(8,128)(2,1)}), bf16[16,52,2048]{2,1,0:T(8,128)(2,1)}, u32[]{:S(2)}, u32[]{:S(2)}) async-start(bf16[16,52,2048]{2,1,0:T(8,128)(2,1)} %reshape.98), calls=%async_computation | async-start | bytes 7340032 | tf_op jit(solution)/shard_map/all_to_all | solution.py:75
  30.6 3.8 copy-start.3
  30.7 190.1 %all-reduce.6.cloned.1.call-start = ((), (), s32[]{:S(2)}) async-start(), calls=%async_computation.7 | async-start | bytes 9437184 | tf_op jit(solution)/shard_map/psum | solution.py:13
  31.5 2.9 copy-start.6
  104.1 4.5 copy-start.7
  108.7 3.0 copy-start.25
  108.7 3.9 copy-start.11
  111.7 0.8 copy-start.23
  120.8 5.1 copy-start.19
  120.8 108.8 %all-to-all-start.1 = ((bf16[16,52,2048]{2,1,0:T(8,128)(2,1)}), bf16[16,52,2048]{2,1,0:T(8,128)(2,1)}, u32[]{:S(2)}, u32[]{:S(2)}) async-start(bf16[16,52,2048]{2,1,0:T(8,128)(2,1)} %reshape.100), calls=%async_computation.1 | async-start | bytes 7340032 | tf_op jit(solution)/shard_map/all_to_all | solution.py:85
  220.8 2.2 copy-start.13
  222.9 1.2 copy-start.2
  222.9 1.7 copy-start.10
  245.3 73.1 %all-to-all-start.2 = ((bf16[16,52,2048]{2,1,0:T(8,128)(2,1)}), bf16[16,52,2048]{2,1,0:T(8,128)(2,1)}, u32[]{:S(2)}, u32[]{:S(2)}) async-start(bf16[16,52,2048]{2,1,0:T(8,128)(2,1)} %reshape.101), calls=%async_computation.2 | async-start | bytes 7340032 | tf_op jit(solution)/shard_map/all_to_all | solution.py:104
  249.8 166.7 %all-reduce.4.cloned.1.call-start = ((), (), s32[]{:S(2)}) async-start(), calls=%async_computation.5 | async-start | bytes 9437184 | tf_op jit(solution)/shard_map/psum | solution.py:133
  249.9 1.4 copy-start.5
  254.9 68.1 %copy-start.24 = (bf16[832,384]{1,0:T(8,128)(2,1)S(1)}, bf16[832,384]{1,0:T(8,128)(2,1)}, u32[]{:S(2)}) copy-start(bf16[832,384]{1,0:T(8,128)(2,1)} %copy-done.23) | copy-start | bytes 1916932
  254.9 321.0 %reduce-scatter.2.cloned.1.call-start = ((), (), s32[]{:S(2)}) async-start(), calls=%async_computation.6 | async-start | bytes 10616832 | tf_op jit(solution)/shard_map/reduce_scatter | solution.py:134
  322.9 6.2 %copy-start.9 = (bf16[832,2048]{1,0:T(8,128)(2,1)S(1)}, bf16[832,2048]{1,0:T(8,128)(2,1)}, u32[]{:S(2)}) copy-start(bf16[832,2048]{1,0:T(8,128)(2,1)} %reshape.102) | copy-start | bytes 10223620
  322.9 6.2 %copy-start.12 = (bf16[1,2048,384]{2,1,0:T(8,128)(2,1)S(1)}, bf16[1,2048,384]{2,1,0:T(8,128)(2,1)}, u32[]{:S(2)}) copy-start(bf16[1,2048,384]{2,1,0:T(8,128)(2,1)} %param.12) | copy-start | bytes 4718596
  322.9 6.2 %copy-start.26 = (f32[832,384]{1,0:T(8,128)S(1)}, f32[832,384]{1,0:T(8,128)}, u32[]{:S(2)}) copy-start(f32[832,384]{1,0:T(8,128)} %copy-done.25) | copy-start | bytes 3833860
  323.0 6.2 %copy-start.27 = (f32[832,384]{1,0:T(8,128)S(1)}, f32[832,384]{1,0:T(8,128)}, u32[]{:S(2)}) copy-start(f32[832,384]{1,0:T(8,128)} %get-tuple-element.36) | copy-start | bytes 3833860
  329.1 2.3 copy-start.8
  331.4 4.0 copy-start.16
  426.0 3.5 copy-start.4
  426.0 3.5 copy-start.17
  437.9 71.3 %all-to-all-start.3 = ((bf16[16,52,2048]{2,1,0:T(8,128)(2,1)}), bf16[16,52,2048]{2,1,0:T(8,128)(2,1)}, u32[]{:S(2)}, u32[]{:S(2)}) async-start(bf16[16,52,2048]{2,1,0:T(8,128)(2,1)} %reshape.103), calls=%async_computation.3 | async-start | bytes 7340032 | tf_op jit(solution)/shard_map/all_to_all | solution.py:119
  443.2 2.9 copy-start.15
  446.2 1.4 copy-start.14
  447.6 2.2 copy-start.18
  447.6 4.0 copy-start.21
  447.6 4.0 copy-start.22
  513.8 64.4 %copy-start.1 = (bf16[256,2048]{1,0:T(8,128)(2,1)S(1)}, bf16[256,2048]{1,0:T(8,128)(2,1)}, u32[]{:S(2)}) copy-start(bf16[256,2048]{1,0:T(8,128)(2,1)} %param.7) | copy-start | bytes 3145732
Sparse Core Ops, SparseCore 0:
  36.7 184.0 all-reduce.5
  255.0 161.5 all-reduce.3
  426.1 149.7 reduce-scatter.1
where the time goes:
time: 592 us; the launch traced here: 585 us
  waiting for transfers between devices  400 us (68%)
  matrix products  74.5 us (13%)
  local copies, waits for them, and re-layouts  46.2 us (8%)
  other arithmetic  29.2 us (5%)
  starting transfers between devices  20.1 us (3%)
  between operations  15.1 us (3%)
    psum x1, waiting for transfers between devices, broadcast(): return lax.psum(kept, axis)  92.6 us
    psum x1, waiting for transfers between devices, per_device(): lax.psum(hot_part.astype(jnp.bfloat16), 'expert').astype(jnp.float32)  77.1 us
    all_to_all x1, waiting for transfers between devices, per_device(): lax.all_to_all(outgoing_grad.reshape(experts, capacity, D), 'expert', spl...  63.2 us
    all_to_all x1, waiting for transfers between devices, per_device(): lax.all_to_all(outgoing, 'expert', split_axis=0, concat_axis=0, tiled=True)  62.9 us
    reduce_scatter x1, waiting for transfers between devices, per_device(): lax.psum_scatter(own_part + jnp.where(is_owner, hot_total, 0.0), 'dp', sc...  57.2 us
    all_to_all x1, waiting for transfers between devices, per_device(): lax.all_to_all(input_rows.reshape(experts, capacity, D), 'expert', split_...  46.8 us
  transfers between devices with their start and end apart: 7, of which 6 were waited for; matrix products, arithmetic and copies ran while one was open for 17% of the time, Pallas kernels for 0%

commit v1 on v0

--- a/solution.py
+++ b/solution.py
@@ -130,7 +130,9 @@
     own_part = jnp.stack([own_gate, own_upper, own_down])
     hot_part = jnp.stack([hot_gate_grad, hot_upper_grad, hot_down_grad])
     is_owner = lax.axis_index("expert") == hot_expert
-    hot_total = lax.psum(hot_part.astype(jnp.bfloat16), "expert").astype(jnp.float32)
+    hot_total = jnp.sum(lax.all_gather(hot_part.astype(jnp.bfloat16), "expert"), axis=0).astype(
+        jnp.float32
+    )
     grads = lax.psum_scatter(
         own_part + jnp.where(is_owner, hot_total, 0.0), "dp", scatter_dimension=1, tiled=True
     )

time: 592 us -> 864 us (1.46)
  blocking collectives: 0 us -> 178 us
  waiting for transfers between devices: 400 us -> 476 us
  other arithmetic: 29.2 us -> 52.9 us
  starting transfers between devices: 20.1 us -> 10.7 us
    all_to_all x0 -> x2, blocking collectives: none -> 178 us  [the longest x1 89.3 us: per_device(): lax.all_to_all(outgoing, 'expert', split_axis=0, concat_axis=0, tiled=True)]
    all_gather x0 -> x1, waiting for transfers between devices: none -> 147 us  [per_device(): lax.all_gather(hot_part.astype(jnp.bfloat16), 'expert')]
    all_to_all x2 -> x0, waiting for transfers between devices: 126 us -> none  [the longest x1 63.2 us: per_device(): lax.all_to_all(outgoing_grad.reshape(experts, capacity, D), 'expert', spl...]
    all_to_all x1, waiting for transfers between devices: 0.01 us -> 82 us  [per_device(): lax.all_to_all(expert_out, 'expert', split_axis=0, concat_axis=0, tiled=T...]
    psum x1 -> x0, waiting for transfers between devices: 77.1 us -> none  [per_device(): lax.psum(hot_part.astype(jnp.bfloat16), 'expert').astype(jnp.float32)]
    psum x1, waiting for transfers between devices: 92.6 us -> 141 us  [broadcast(): return lax.psum(kept, axis)]
    reduce_sum x0 -> x1, other arithmetic: none -> 26.4 us  [per_device(): jnp.sum(lax.all_gather(hot_part.astype(jnp.bfloat16), 'expert'), axis=0)]
    all_to_all x2 -> x0, starting transfers between devices: 10.2 us -> none  [the longest x1 5.66 us: per_device(): lax.all_to_all(outgoing, 'expert', split_axis=0, concat_axis=0, tiled=True)]
  transfers between devices with their start and end apart: 7 -> 5, of which waited for: 6 -> 5; matrix products, arithmetic and copies ran while one was open for 17% -> 13% of each run, Pallas kernels for 0% -> 0%
where the time goes in v1:
time: 864 us; the launch traced here: 856 us
  waiting for transfers between devices  476 us (55%)
  blocking collectives  178 us (21%)
  matrix products  71.8 us (8%)
  other arithmetic  52.9 us (6%)
  local copies, waits for them, and re-layouts  52 us (6%)
  between operations  15 us (2%)
  starting transfers between devices  10.7 us (1%)
    all_gather x1, waiting for transfers between devices, per_device(): lax.all_gather(hot_part.astype(jnp.bfloat16), 'expert')  147 us
    psum x1, waiting for transfers between devices, broadcast(): return lax.psum(kept, axis)  141 us
    all_to_all x1, blocking collectives, per_device(): lax.all_to_all(outgoing, 'expert', split_axis=0, concat_axis=0, tiled=True)  89.3 us
    all_to_all x1, blocking collectives, per_device(): lax.all_to_all(outgoing_grad.reshape(experts, capacity, D), 'expert', spl...  89 us
    all_to_all x1, waiting for transfers between devices, per_device(): lax.all_to_all(expert_out, 'expert', split_axis=0, concat_axis=0, tiled=T...  82 us
    reduce_scatter x1, waiting for transfers between devices, per_device(): lax.psum_scatter(own_part + jnp.where(is_owner, hot_total, 0.0), 'dp', sc...  59 us
    all_to_all x1, waiting for transfers between devices, per_device(): lax.all_to_all(input_rows.reshape(experts, capacity, D), 'expert', split_...  47 us
    reduce_sum x1, other arithmetic, per_device(): jnp.sum(lax.all_gather(hot_part.astype(jnp.bfloat16), 'expert'), axis=0)  26.4 us
  transfers between devices with their start and end apart: 5, of which 5 were waited for; matrix products, arithmetic and copies ran while one was open for 13% of the time, Pallas kernels for 0%

profile of v1, /device:TPU:0, one launch (start us, length us, event | category | flops | bytes accessed | tf_op | source)
XLA Modules:
  0.0 856.5 jit_solution(15552599443730830953)
XLA Ops:
  7.2 1.0 convert_reduce_fusion.1
  9.5 2.8 bitcast_select_fusion
  12.4 2.0 bitcast_select_fusion.1
  15.8 141.1 %all-reduce.3.cloned.1.call-done = (bf16[2048,384]{1,0:T(8,128)(2,1)}, bf16[2048,384]{1,0:T(8,128)(2,1)}, bf16[2048,384]{1,0:T(8,128)(2,1)}) async-done(((bf16[2048,384]{1,0:T(8,128)(2,1)}, bf16[2048,384]{1,0:T(8,128)(2,1)}, bf16[2048,384]{1,0:T(8,128)(2,1)}), (bf16[2048,384]{1,0:T(8,128)(2,1)}, bf16[2048,384]{1,0:T(8,128)(2,1)}, bf16[2048,384]{1,0:T(8,128)(2,1)})) %all-reduce.3.cloned.1.call-update) | async-done | bytes 4718608 | tf_op jit(solution)/shard_map/psum | solution.py:13
  156.9 2.1 convolution_bitcast_fusion.3
  160.7 1.0 multiply_convert_fusion.4
  162.9 0.7 fusion.10
  163.6 2.4 pad_maximum_fusion
  166.0 6.6 copy.80
  173.0 4.5 reduce-window.6
  178.8 2.9 convolution_convert_fusion.1
  181.6 5.1 reshape.146
  186.8 89.3 %all_to_all.20 = bf16[16,52,2048]{2,1,0:T(8,128)(2,1)} all-to-all(bf16[16,52,2048]{2,1,0:T(8,128)(2,1)} %reshape.146), channel_id=1, replica_groups=mesh['dp'=8,'expert'=16] {'expert'}, dimensions={0} | all-to-all | bytes 6815744 | tf_op jit(solution)/shard_map/all_to_all | solution.py:75
  276.0 4.7 reshape.147
  280.7 4.5 fusion.28
  285.2 3.0 multiply_convert_fusion.3
  288.3 3.8 convolution_convert_fusion
  292.0 4.6 reshape.148
  296.6 4.6 all-to-all-start.1
  302.0 1.6 fusion.30
  303.6 82.0 %all-to-all-done.1 = bf16[16,52,2048]{2,1,0:T(8,128)(2,1)} async-done(((bf16[16,52,2048]{2,1,0:T(8,128)(2,1)}), bf16[16,52,2048]{2,1,0:T(8,128)(2,1)}, u32[]{:S(2)}, u32[]{:S(2)}) %all-to-all-start.1) | async-done | bytes 3407904 | tf_op jit(solution)/shard_map/all_to_all | solution.py:85
  385.6 5.4 reshape.153
  391.0 5.9 multiply_reduce_fusion
  396.9 4.5 reshape.149
  401.5 89.0 %all_to_all.21 = bf16[16,52,2048]{2,1,0:T(8,128)(2,1)} all-to-all(bf16[16,52,2048]{2,1,0:T(8,128)(2,1)} %reshape.149), channel_id=1, replica_groups=mesh['dp'=8,'expert'=16] {'expert'}, dimensions={0} | all-to-all | bytes 6815744 | tf_op jit(solution)/shard_map/all_to_all | solution.py:104
  490.5 4.6 reshape.150
  495.1 6.1 convolution_bitcast_fusion
  501.3 2.3 multiply_convert_fusion.1
  503.6 4.0 convolution_bitcast_fusion.1
  507.6 4.0 convolution_bitcast_fusion.2
  511.6 146.8 %all-gather.2.cloned.1.call-done = bf16[16,3,2048,384]{3,2,1,0:T(8,128)(2,1)} async-done(((bf16[1,3,2048,384]{3,2,1,0:T(8,128)(2,1)}), bf16[16,3,2048,384]{3,2,1,0:T(8,128)(2,1)}) %all-gather.2.cloned.1.call-update) | async-done | bytes 75497488 | tf_op jit(solution)/shard_map/all_gather | solution.py:133
  658.4 26.4 %reduce_sum.75 = bf16[3,2048,384]{2,1,0:T(8,128)(2,1)} reduce(bf16[16,3,2048,384]{3,2,1,0:T(8,128)(2,1)} %all-gather.2.cloned.1.call-done, bf16[]{:T(256)} %constant.30.clone.1), dimensions={0}, to_apply=%region_12.13 | reduce | flops 35389440 | bytes 80216064 | tf_op jit(solution)/shard_map/reduce_sum | solution.py:133
  684.8 9.4 %maximum_add_fusion = f32[3,2048,384]{2,1,0:T(8,128)} fusion(f32[1,2048,384]{2,1,0:T(8,128)} %convolution_bitcast_fusion, f32[1,2048,384]{2,1,0:T(8,128)} %convolution_bitcast_fusion.1, f32[1,2048,384]{2,1,0:T(8,128)} %convolution_bitcast_fusion.2, bf16[3,2048,384]{2,1,0:T(8,128)(2,1)} %reduce_sum.75, pred[]{:T(512)S(6)} %eq.93), kind=kLoop, calls=%fused_computation | loop fusion | flops 11796480 | bytes 23592960 | tf_op jit(solution)/shard_map/add | solution.py:137
  694.2 3.5 fusion.26
  697.8 3.7 add_convert_fusion
  701.4 4.6 reshape.151
  706.1 5.9 all-to-all-start.3
  712.0 0.8 copy.78
  712.8 2.9 fusion.18
  715.7 0.7 fusion.43
  717.2 2.1 fusion.16
  719.3 1.7 select_reduce_fusion
  721.7 10.3 %fusion.11 = bf16[256,2048]{1,0:T(8,128)(2,1)} fusion(f32[832,256]{1,0:T(8,128)S(1)} %convert_reduce_fusion, f32[832,2048]{1,0:T(8,128)} %reshape.153, f32[832]{0:T(1024)S(1)} %fusion.30, bf16[256,2048]{1,0:T(8,128)(2,1)S(1)} %get-tuple-element.44, f32[256]{0:T(256)S(1)} %get-tuple-element.29), kind=kOutput, calls=%fused_computation.32 | convolution fusion | flops 5238292480 | bytes 9769216 | tf_op jit(solution)/shard_map/dot_general | solution.py:89
  731.9 47.0 %all-to-all-done.3 = bf16[16,52,2048]{2,1,0:T(8,128)(2,1)} async-done(((bf16[16,52,2048]{2,1,0:T(8,128)(2,1)}), bf16[16,52,2048]{2,1,0:T(8,128)(2,1)}, u32[]{:S(2)}, u32[]{:S(2)}) %all-to-all-start.3) | async-done | bytes 3407904 | tf_op jit(solution)/shard_map/all_to_all | solution.py:119
  778.9 4.6 reshape.152
  783.5 4.9 fusion.14
  788.5 59.0 %reduce-scatter.2.cloned.1.call-done = f32[3,256,384]{2,1,0:T(8,128)} async-done(((f32[3,2048,384]{2,1,0:T(8,128)}), f32[3,256,384]{2,1,0:T(8,128)}) %reduce-scatter.2.cloned.1.call-update) | async-done | bytes 1179664 | tf_op jit(solution)/shard_map/reduce_scatter | solution.py:136
  847.5 2.3 fusion.42
  (91 shorter events, 8.6 us)
Async XLA Ops:
  7.2 149.7 %copy-start = (bf16[256,2048]{1,0:T(8,128)(2,1)S(1)}, bf16[256,2048]{1,0:T(8,128)(2,1)}, u32[]{:S(2)}) copy-start(bf16[256,2048]{1,0:T(8,128)(2,1)} %param.7) | copy-start | bytes 3145732
  7.2 5.2 copy-start.3
  7.2 149.7 %all-reduce.3.cloned.1.call-start = ((), (), s32[]{:S(2)}) async-start(), calls=%async_computation.7 | async-start | bytes 9437184 | tf_op jit(solution)/shard_map/psum | solution.py:13
  9.5 2.8 copy-start.6
  14.4 0.7 copy-start.19
  14.4 0.7 copy-start.20
  14.4 644.0 %all-gather.2.cloned.1.call-start = ((), (), s32[]{:S(2)}) async-start(), calls=%async_computation.5 | async-start | bytes 80216064 | tf_op jit(solution)/shard_map/all_gather | solution.py:133
  15.8 162.5 %copy-start.22 = (pred[256,4]{0,1:T(4,128)(4,1)}, pred[256,4]{0,1:T(4,128)(4,1)S(1)}, u32[]{:S(2)}) copy-start(pred[256,4]{0,1:T(4,128)(4,1)S(1)} %get-tuple-element.30) | copy-start | bytes 3076
  156.8 2.2 copy-start.14
  159.0 1.2 copy-start.2
  159.0 1.7 copy-start.10
  280.7 4.5 copy-start.4
  280.7 4.5 copy-start.7
  285.2 3.0 copy-start.26
  285.2 3.0 copy-start.11
  296.6 4.7 copy-start.23
  296.6 4.9 copy-start.21
  296.6 89.0 %all-to-all-start.1 = ((bf16[16,52,2048]{2,1,0:T(8,128)(2,1)}), bf16[16,52,2048]{2,1,0:T(8,128)(2,1)}, u32[]{:S(2)}, u32[]{:S(2)}) async-start(bf16[16,52,2048]{2,1,0:T(8,128)(2,1)} %reshape.148), calls=%async_computation.1 | async-start | bytes 7340032 | tf_op jit(solution)/shard_map/all_to_all | solution.py:85
  301.3 546.2 %reduce-scatter.2.cloned.1.call-start = ((), (), s32[]{:S(2)}) async-start(), calls=%async_computation.6 | async-start | bytes 10616832 | tf_op jit(solution)/shard_map/reduce_scatter | solution.py:136
  495.1 6.2 copy-start.9
  495.1 6.2 copy-start.12
  495.1 6.2 copy-start.27
  495.1 6.2 copy-start.28
  501.3 2.3 copy-start.8
  503.6 4.0 copy-start.16
  694.2 3.5 copy-start.5
  694.2 3.5 copy-start.17
  706.1 72.8 %all-to-all-start.3 = ((bf16[16,52,2048]{2,1,0:T(8,128)(2,1)}), bf16[16,52,2048]{2,1,0:T(8,128)(2,1)}, u32[]{:S(2)}, u32[]{:S(2)}) async-start(bf16[16,52,2048]{2,1,0:T(8,128)(2,1)} %reshape.151), calls=%async_computation.3 | async-start | bytes 7340032 | tf_op jit(solution)/shard_map/all_to_all | solution.py:119
  712.8 2.9 copy-start.15
  715.7 1.4 copy-start.13
  717.1 2.1 copy-start.18
  717.1 3.9 copy-start.24
  717.1 3.9 copy-start.25
  783.5 66.2 %copy-start.1 = (bf16[256,2048]{1,0:T(8,128)(2,1)S(1)}, bf16[256,2048]{1,0:T(8,128)(2,1)}, u32[]{:S(2)}) copy-start(bf16[256,2048]{1,0:T(8,128)(2,1)} %param.7) | copy-start | bytes 3145732
Sparse Core Ops, SparseCore 0:
  14.5 142.2 all-reduce.2
  172.8 485.5 all-gather.1
  694.3 153.0 reduce-scatter.1
